TPU v7x, 32 devices: a whole 2x2x4 slice. The times are simulated.
32 devices in a mesh: expert: 4 (over y, x), shard: 8 (over z, core).
Axes of the slice: x: 2, y: 2, z: 4, core: 2. Of those that a mesh axis runs over, the one named last changes fastest.
Arguments:
- hidden: bfloat16 [64, 4096], P('shard'), may hold values from -6 to 6
- queries: bfloat16 [64, 32, 128], P('shard', 'expert'), may hold values from -30 to 30
- key_cache: bfloat16 [64, 512, 8, 128], P('shard', None, 'expert'), may hold values from -16 to 16
- value_cache: bfloat16 [64, 512, 8, 128], P('shard', None, 'expert'), may hold values from -6 to 6
- out_weight: bfloat16 [4096, 4096], P('expert', 'shard'), may hold values from -0.09375 to 0.09375
- norm_gain: bfloat16 [4096], replicated, may hold values from 0.099609375 to 1.8984375
- router: bfloat16 [4096, 8], replicated, may hold values from -0.09375 to 0.09375
- expert_ids: int32 [64, 2], replicated, may hold values from 0 to 7, all different within a row; in each aligned block of 64 rows (0 to 63, 64 to 127, ...) at most 32 rows name the same one
- gate_weight: bfloat16 [8, 4096, 14336], P('expert', None, 'shard'), may hold values from -0.09375 to 0.09375
- up_weight: bfloat16 [8, 4096, 14336], P('expert', None, 'shard'), may hold values from -0.09375 to 0.09375
- down_weight: bfloat16 [8, 14336, 4096], P('expert', 'shard'), may hold values from -0.046875 to 0.046875
Outputs:
- layer_out: bfloat16 [64, 4096], P('shard')
Inputs may be any that keep to these rules, and one draw needn't show every extreme that they name: `expert_ids`: each token names two different experts; over all 64 tokens no expert is named by more than 32 tokens, a bound that some block reaches.
All inputs are finite; a program needn't handle non-finite values.
Results may differ from a plain program's by a relative error of at most 0.008.
Values may be sent and summed in bfloat16 or wider, within the bound.
A program may use at most 128 MiB of HBM per device.

v0:
```python
import math
import jax
import jax.numpy as jnp
from jax import lax
from jax.sharding import PartitionSpec as P


def on_device(
    hidden,
    queries,
    key_cache,
    value_cache,
    out_weight,
    norm_gain,
    router,
    expert_ids,
    gate_weight,
    up_weight,
    down_weight,
):
    count_local, heads_local, head_size = queries.shape
    kv_local = key_cache.shape[2]
    per_kv = heads_local // kv_local
    query_blocks = queries.reshape(count_local, kv_local, per_kv, head_size)
    scores = jnp.einsum(
        "tkgd,tpkd->tkgp", query_blocks, key_cache, preferred_element_type=jnp.float32
    ) / math.sqrt(head_size)
    attn_weights = jax.nn.softmax(scores, axis=-1).astype(jnp.bfloat16)
    attended = jnp.einsum(
        "tkgp,tpkd->tkgd", attn_weights, value_cache, preferred_element_type=jnp.float32
    )
    attended = attended.astype(jnp.bfloat16).reshape(count_local, heads_local * head_size)
    all_attended = lax.all_gather(attended, "shard", axis=0, tiled=True)
    partial_cols = jnp.dot(all_attended, out_weight, preferred_element_type=jnp.float32)
    partial_heads = lax.all_to_all(partial_cols, "shard", split_axis=0, concat_axis=1, tiled=True)
    attn_out = lax.psum(partial_heads, "expert")
    stream = hidden.astype(jnp.float32) + attn_out
    scaled = stream * lax.rsqrt(jnp.mean(stream * stream, axis=-1, keepdims=True) + 1e-05)
    normed = (scaled * norm_gain.astype(jnp.float32)).astype(jnp.bfloat16)
    everyone = lax.all_gather(normed, "shard", axis=0, tiled=True)
    token_count = everyone.shape[0]
    logits = jnp.dot(everyone, router, preferred_element_type=jnp.float32)
    top_first = jnp.take_along_axis(logits, expert_ids[:, 0:1], axis=1)[:, 0]
    top_second = jnp.take_along_axis(logits, expert_ids[:, 1:2], axis=1)[:, 0]
    weight_first = 1.0 / (1.0 + jnp.exp(top_second - top_first))
    weight_second = 1.0 / (1.0 + jnp.exp(top_first - top_second))
    local_experts = gate_weight.shape[0]
    group_index = lax.axis_index("expert")
    summed = jnp.zeros((token_count, everyone.shape[1]), jnp.float32)
    for member in range(local_experts):
        expert = group_index * local_experts + member
        in_first = expert_ids[:, 0] == expert
        in_second = expert_ids[:, 1] == expert
        routed_weight = jnp.where(in_first, weight_first, 0.0) + jnp.where(
            in_second, weight_second, 0.0
        )
        gated = jnp.dot(everyone, gate_weight[member], preferred_element_type=jnp.float32)
        upward = jnp.dot(everyone, up_weight[member], preferred_element_type=jnp.float32)
        activated = (jax.nn.silu(gated) * upward).astype(jnp.bfloat16)
        expert_out = jnp.dot(activated, down_weight[member], preferred_element_type=jnp.float32)
        summed = summed + routed_weight[:, None] * expert_out
    reduced = lax.psum_scatter(summed, "shard", scatter_dimension=0, tiled=True)
    expert_mix = lax.psum(reduced, "expert")
    return (stream + expert_mix).astype(jnp.bfloat16)


def solution(mesh):
    in_specs = (
        P("shard", None),
        P("shard", "expert", None),
        P("shard", None, "expert", None),
        P("shard", None, "expert", None),
        P("expert", "shard"),
        P(),
        P(),
        P(),
        P("expert", None, "shard"),
        P("expert", None, "shard"),
        P("expert", "shard", None),
    )
    out_specs = P("shard", None)
    return jax.shard_map(
        on_device, mesh=mesh, in_specs=in_specs, out_specs=out_specs, check_vma=False
    )
```

profile of v0, /device:TPU:0, one launch (start us, length us, event | category | flops | bytes accessed | tf_op | source)
XLA Modules:
  0.0 225.8 jit_solution(6295233523832174419)
XLA Ops:
  6.5 1.6 copy-done
  8.1 1.4 fusion.46
  9.5 0.2 fusion.79
  9.7 2.0 fusion.49
  11.8 15.7 %all_gather.6 = bf16[64,1024]{1,0:T(8,128)(2,1)S(1)} all-gather(bf16[8,1024]{1,0:T(8,128)(2,1)S(1)} %reshape.37), channel_id=1, replica_groups=mesh['expert'=4,'shard'=8] {'shard'}, dimensions={0}, use_global_device_ids=true | all-gather | bytes 147456 | tf_op jit(solution)/shard_map/all_gather | solution.py:33
  27.5 2.2 convolution_bitcast_fusion
  29.7 4.6 %all-to-all-start = ((f32[8,8,512]{2,1,0:T(8,128)}), f32[8,8,512]{2,1,0:T(8,128)S(1)}, u32[]{:S(2)}, u32[]{:S(2)}) async-start(f32[8,8,512]{2,1,0:T(8,128)} %convolution_bitcast_fusion), calls=%async_computation | async-start | bytes 262144 | tf_op jit(solution)/shard_map/all_to_all | solution.py:35
  34.3 0.0 all-reduce.3.cloned.1.call-start
  34.3 0.7 convert_element_type.27
  35.0 0.8 fusion.78
  35.8 5.2 %all-to-all-done = f32[8,8,512]{2,1,0:T(8,128)S(1)} async-done(((f32[8,8,512]{2,1,0:T(8,128)}), f32[8,8,512]{2,1,0:T(8,128)S(1)}, u32[]{:S(2)}, u32[]{:S(2)}) %all-to-all-start) | async-done | bytes 131104 | tf_op jit(solution)/shard_map/all_to_all | solution.py:35
  41.0 0.6 copy-done.4
  41.7 0.0 all-reduce.3.cloned.1.call-update
  41.7 0.0 reduce-scatter.2.cloned.1.call-start
  41.8 41.4 %all-reduce.3.cloned.1.call-done = f32[8,4096]{1,0:T(8,128)} async-done(((f32[8,4096]{1,0:T(8,128)}), f32[8,4096]{1,0:T(8,128)}) %all-reduce.3.cloned.1.call-update) | async-done | bytes 131088 | tf_op jit(solution)/shard_map/psum | solution.py:36
  83.2 1.1 multiply_reduce_fusion
  84.2 1.0 multiply_convert_fusion
  85.2 14.7 %all_gather.7 = bf16[64,4096]{1,0:T(8,128)(2,1)S(1)} all-gather(bf16[8,4096]{1,0:T(8,128)(2,1)S(1)} %multiply_convert_fusion), channel_id=1, replica_groups=mesh['expert'=4,'shard'=8] {'shard'}, dimensions={0}, use_global_device_ids=true | all-gather | bytes 589824 | tf_op jit(solution)/shard_map/all_gather | solution.py:40
  100.0 6.5 %fusion.5 = f32[64,1792]{1,0:T(8,128)S(1)} fusion(bf16[64,4096]{1,0:T(8,128)(2,1)S(1)} %all_gather.7, bf16[2,4096,1792]{2,1,0:T(8,128)(2,1)} %param.21), kind=kOutput, calls=%fused_computation.7 | convolution fusion | flops 939524096 | bytes 15663104 | tf_op jit(solution)/shard_map/dot_general | solution.py:57
  106.4 6.4 %fusion.11 = f32[64,1792]{1,0:T(8,128)S(1)} fusion(bf16[64,4096]{1,0:T(8,128)(2,1)S(1)} %all_gather.7, bf16[2,4096,1792]{2,1,0:T(8,128)(2,1)} %param.21), kind=kOutput, calls=%fused_computation.13 | convolution fusion | flops 939524096 | bytes 15663104 | tf_op jit(solution)/shard_map/dot_general | solution.py:57
  112.9 0.2 fusion.80
  113.2 0.7 gather_fusion
  113.9 0.7 gather_fusion.1
  114.7 13.1 %fusion.25 = f32[64,4096]{1,0:T(8,128)} fusion(bf16[2,1792,4096]{2,1,0:T(8,128)(2,1)} %param.23, bf16[64,4096]{1,0:T(8,128)(2,1)S(1)} %all_gather.7, bf16[2,4096,1792]{2,1,0:T(8,128)(2,1)} %param.22, f32[64]{0:T(128)S(1)} %fusion.73, f32[64,1792]{1,0:T(8,128)S(1)} %fusion.5), kind=kOutput, calls=%fused_computation.23 | convolution fusion | flops 1879998464 | bytes 31392000 | tf_op jit(solution)/shard_map/dot_general | solution.py:60
  127.8 13.6 %fusion.22 = f32[64,4096]{1,0:T(8,128)} fusion(f32[64,4096]{1,0:T(8,128)} %fusion.25, bf16[2,1792,4096]{2,1,0:T(8,128)(2,1)} %param.23, bf16[64,4096]{1,0:T(8,128)(2,1)S(1)} %all_gather.7, bf16[2,4096,1792]{2,1,0:T(8,128)(2,1)} %param.22, f32[64]{0:T(128)S(1)} %get-tuple-element.6, f32[64,1792]{1,0:T(8,128)S(1)} %fusion.11), kind=kOutput, calls=%fused_computation.22 | convolution fusion | flops 1880260608 | bytes 32440576 | tf_op jit(solution)/shard_map/dot_general | solution.py:60
  141.4 0.0 reduce-scatter.2.cloned.1.call-update
  141.5 0.0 all-reduce.5.cloned.1.call-start
  141.5 32.9 %reduce-scatter.2.cloned.1.call-done = f32[8,4096]{1,0:T(8,128)} async-done(((f32[64,4096]{1,0:T(8,128)}), f32[8,4096]{1,0:T(8,128)}) %reduce-scatter.2.cloned.1.call-update) | async-done | bytes 131088 | tf_op jit(solution)/shard_map/reduce_scatter | solution.py:62
  174.4 0.0 all-reduce.5.cloned.1.call-update
  174.4 43.3 %all-reduce.5.cloned.1.call-done = f32[8,4096]{1,0:T(8,128)} async-done(((f32[8,4096]{1,0:T(8,128)}), f32[8,4096]{1,0:T(8,128)}) %all-reduce.5.cloned.1.call-update) | async-done | bytes 131088 | tf_op jit(solution)/shard_map/psum | solution.py:63
  217.7 1.6 add_convert_fusion
  219.2 0.0 copy-done.1
  (19 shorter events, 0.1 us)
Async XLA Ops:
  6.5 1.6 copy-start
  29.7 11.3 %all-to-all-start = ((f32[8,8,512]{2,1,0:T(8,128)}), f32[8,8,512]{2,1,0:T(8,128)S(1)}, u32[]{:S(2)}, u32[]{:S(2)}) async-start(f32[8,8,512]{2,1,0:T(8,128)} %convolution_bitcast_fusion), calls=%async_computation | async-start | bytes 262144 | tf_op jit(solution)/shard_map/all_to_all | solution.py:35
  34.3 48.9 %all-reduce.3.cloned.1.call-start = ((), (), s32[]{:S(2)}) async-start(), calls=%async_computation.2 | async-start | bytes 262144 | tf_op jit(solution)/shard_map/psum | solution.py:36
  41.0 0.6 copy-start.4
  41.7 132.7 %reduce-scatter.2.cloned.1.call-start = ((), (), s32[]{:S(2)}) async-start(), calls=%async_computation.3 | async-start | bytes 1179648 | tf_op jit(solution)/shard_map/reduce_scatter | solution.py:62
  100.0 12.9 %copy-start.5 = (bf16[4096,8]{0,1:T(8,128)(2,1)S(1)}, bf16[4096,8]{0,1:T(8,128)(2,1)}, u32[]{:S(2)}) copy-start(bf16[4096,8]{0,1:T(8,128)(2,1)} %param.19) | copy-start | bytes 196612
  100.0 14.7 %copy-start.6 = (s32[64,2]{0,1:T(2,128)S(1)}, s32[64,2]{0,1:T(2,128)}, u32[]{:S(2)}) copy-start(s32[64,2]{0,1:T(2,128)} %param.20) | copy-start | bytes 1540
  127.8 91.4 %copy-start.1 = (bf16[8,512,2,128]{3,2,1,0:T(2,128)(2,1)S(1)}, bf16[8,512,2,128]{3,2,1,0:T(2,128)(2,1)}, u32[]{:S(2)}) copy-start(bf16[8,512,2,128]{3,2,1,0:T(2,128)(2,1)} %param.15) | copy-start | bytes 6291460
  127.8 89.9 %copy-start.2 = (f32[8,4096]{1,0:T(8,128)S(1)}, f32[8,4096]{1,0:T(8,128)}, u32[]{:S(2)}) copy-start(f32[8,4096]{1,0:T(8,128)} %all-reduce.3.cloned.1.call-done) | copy-start | bytes 393220
  127.8 89.9 %copy-start.3 = (bf16[8,4096]{1,0:T(8,128)(2,1)S(1)}, bf16[8,4096]{1,0:T(8,128)(2,1)}, u32[]{:S(2)}) copy-start(bf16[8,4096]{1,0:T(8,128)(2,1)} %param.13) | copy-start | bytes 196612
  141.5 76.2 %all-reduce.5.cloned.1.call-start = ((), (), s32[]{:S(2)}) async-start(), calls=%async_computation.4 | async-start | bytes 262144 | tf_op jit(solution)/shard_map/psum | solution.py:63
Sparse Core Ops, SparseCore 0:
  41.8 41.2 all-reduce.2
  141.6 32.7 reduce-scatter.1
  177.3 40.3 all-reduce.4
where the time goes:
time: 226 us
  waiting for transfers between devices  123 us (54%)
  matrix products  45.5 us (20%)
  blocking collectives  30.5 us (13%)
  between operations  13.2 us (6%)
  other arithmetic  5.35 us (2%)
  starting transfers between devices  4.72 us (2%)
  local copies, waits for them, and re-layouts  3.76 us (2%)
    psum x1, waiting for transfers between devices, on_device(): expert_mix = lax.psum(reduced, 'expert')  43.3 us
    psum x1, waiting for transfers between devices, on_device(): attn_out = lax.psum(partial_heads, 'expert')  41.4 us
    reduce_scatter x1, waiting for transfers between devices, on_device(): reduced = lax.psum_scatter(summed, 'shard', scatter_dimension=0, tiled=True)  32.9 us
    dot_general x2, matrix products, on_device(): jnp.dot(activated, down_weight[member], preferred_element_type=jnp.float32)  26.7 us
    all_gather x1, blocking collectives, on_device(): all_attended = lax.all_gather(attended, 'shard', axis=0, tiled=True)  15.7 us
    all_gather x1, blocking collectives, on_device(): everyone = lax.all_gather(normed, 'shard', axis=0, tiled=True)  14.7 us
    dot_general x2, matrix products, on_device(): jnp.dot(everyone, gate_weight[member], preferred_element_type=jnp.float32)  12.9 us
    all_to_all x1, waiting for transfers between devices, on_device(): lax.all_to_all(partial_cols, 'shard', split_axis=0, concat_axis=1, tiled=...  5.22 us
  transfers between devices with their start and end apart: 4, of which 4 were waited for; matrix products, arithmetic and copies ran while one was open for 1% of the time, Pallas kernels for 0%

commit v1 on v0

--- a/solution.py
+++ b/solution.py
@@ -30,7 +30,14 @@
         "tkgp,tpkd->tkgd", attn_weights, value_cache, preferred_element_type=jnp.float32
     )
     attended = attended.astype(jnp.bfloat16).reshape(count_local, heads_local * head_size)
-    all_attended = lax.all_gather(attended, "shard", axis=0, tiled=True)
+    ring = [attended]
+    for hop in range(7):
+        ring.append(lax.ppermute(ring[-1], "shard", [(dev, (dev + 1) % 8) for dev in range(8)]))
+    all_attended = jnp.roll(
+        jnp.concatenate(ring[::-1], axis=0),
+        (lax.axis_index("shard") + 1) * ring[0].shape[0],
+        axis=0,
+    )
     partial_cols = jnp.dot(all_attended, out_weight, preferred_element_type=jnp.float32)
     partial_heads = lax.all_to_all(partial_cols, "shard", split_axis=0, concat_axis=1, tiled=True)
     attn_out = lax.psum(partial_heads, "expert")

time: 226 us -> 246 us (1.088)
  waiting for transfers between devices: 123 us -> 158 us
  blocking collectives: 30.5 us -> 14.7 us
    ppermute x0 -> x7, waiting for transfers between devices: none -> 34.5 us  [on_device(): lax.ppermute(ring[-1], 'shard', [(dev, (dev + 1) % 8) for dev in range(8)])]
    all_gather x1 -> x0, blocking collectives: 15.7 us -> none  [on_device(): all_attended = lax.all_gather(attended, 'shard', axis=0, tiled=True)]
  transfers between devices with their start and end apart: 4 -> 11, of which waited for: 4 -> 11; matrix products, arithmetic and copies ran while one was open for 1% -> 1% of each run, Pallas kernels for 0% -> 0%
where the time goes in v1:
time: 246 us; the launch traced here: 245 us
  waiting for transfers between devices  158 us (64%)
  matrix products  45.4 us (18%)
  blocking collectives  14.7 us (6%)
  between operations  13.3 us (5%)
  other arithmetic  5.35 us (2%)
  starting transfers between devices  4.06 us (2%)
  local copies, waits for them, and re-layouts  3.81 us (2%)
    psum x1, waiting for transfers between devices, on_device(): expert_mix = lax.psum(reduced, 'expert')  43.4 us
    psum x1, waiting for transfers between devices, on_device(): attn_out = lax.psum(partial_heads, 'expert')  41.9 us
    ppermute x7, waiting for transfers between devices, on_device(): lax.ppermute(ring[-1], 'shard', [(dev, (dev + 1) % 8) for dev in range(8)])  34.5 us
    reduce_scatter x1, waiting for transfers between devices, on_device(): reduced = lax.psum_scatter(summed, 'shard', scatter_dimension=0, tiled=True)  32.9 us
    dot_general x2, matrix products, on_device(): jnp.dot(activated, down_weight[member], preferred_element_type=jnp.float32)  26.7 us
    all_gather x1, blocking collectives, on_device(): everyone = lax.all_gather(normed, 'shard', axis=0, tiled=True)  14.7 us
    dot_general x2, matrix products, on_device(): jnp.dot(everyone, gate_weight[member], preferred_element_type=jnp.float32)  12.9 us
    all_to_all x1, waiting for transfers between devices, on_device(): lax.all_to_all(partial_cols, 'shard', split_axis=0, concat_axis=1, tiled=...  5.86 us
  transfers between devices with their start and end apart: 11, of which 11 were waited for; matrix products, arithmetic and copies ran while one was open for 1% of the time, Pallas kernels for 0%

profile of v1, /device:TPU:0, one launch (start us, length us, event | category | flops | bytes accessed | tf_op | source)
XLA Modules:
  0.0 245.2 jit_solution(613235889628952572)
XLA Ops:
  6.5 1.6 copy-done
  8.1 1.4 fusion.46
  9.5 0.2 fusion.81
  9.7 2.0 fusion.49
  11.8 0.5 collective-permute-start
  12.3 5.4 %collective-permute-done = bf16[8,1024]{1,0:T(8,128)(2,1)S(1)} collective-permute-done((bf16[8,1024]{1,0:T(8,128)(2,1)S(1)}, bf16[8,1024]{1,0:T(8,128)(2,1)S(1)}, u32[]{:S(2)}, u32[]{:S(2)}) %collective-permute-start) | collective-permute-done | bytes 16416 | tf_op jit(solution)/shard_map/ppermute | solution.py:35
  17.8 5.0 %collective-permute-done.1 = bf16[8,1024]{1,0:T(8,128)(2,1)S(1)} collective-permute-done((bf16[8,1024]{1,0:T(8,128)(2,1)S(1)}, bf16[8,1024]{1,0:T(8,128)(2,1)S(1)}, u32[]{:S(2)}, u32[]{:S(2)}) %collective-permute-start.1) | collective-permute-done | bytes 16416 | tf_op jit(solution)/shard_map/ppermute | solution.py:35
  22.7 5.0 %collective-permute-done.2 = bf16[8,1024]{1,0:T(8,128)(2,1)S(1)} collective-permute-done((bf16[8,1024]{1,0:T(8,128)(2,1)S(1)}, bf16[8,1024]{1,0:T(8,128)(2,1)S(1)}, u32[]{:S(2)}, u32[]{:S(2)}) %collective-permute-start.2) | collective-permute-done | bytes 16416 | tf_op jit(solution)/shard_map/ppermute | solution.py:35
  27.7 5.0 %collective-permute-done.3 = bf16[8,1024]{1,0:T(8,128)(2,1)S(1)} collective-permute-done((bf16[8,1024]{1,0:T(8,128)(2,1)S(1)}, bf16[8,1024]{1,0:T(8,128)(2,1)S(1)}, u32[]{:S(2)}, u32[]{:S(2)}) %collective-permute-start.3) | collective-permute-done | bytes 16416 | tf_op jit(solution)/shard_map/ppermute | solution.py:35
  32.7 5.0 %collective-permute-done.4 = bf16[8,1024]{1,0:T(8,128)(2,1)S(1)} collective-permute-done((bf16[8,1024]{1,0:T(8,128)(2,1)S(1)}, bf16[8,1024]{1,0:T(8,128)(2,1)S(1)}, u32[]{:S(2)}, u32[]{:S(2)}) %collective-permute-start.4) | collective-permute-done | bytes 16416 | tf_op jit(solution)/shard_map/ppermute | solution.py:35
  37.6 5.0 %collective-permute-done.5 = bf16[8,1024]{1,0:T(8,128)(2,1)S(1)} collective-permute-done((bf16[8,1024]{1,0:T(8,128)(2,1)S(1)}, bf16[8,1024]{1,0:T(8,128)(2,1)S(1)}, u32[]{:S(2)}, u32[]{:S(2)}) %collective-permute-start.5) | collective-permute-done | bytes 16416 | tf_op jit(solution)/shard_map/ppermute | solution.py:35
  42.6 0.7 convert_element_type.27
  43.3 4.3 %collective-permute-done.6 = bf16[8,1024]{1,0:T(8,128)(2,1)S(1)} collective-permute-done((bf16[8,1024]{1,0:T(8,128)(2,1)S(1)}, bf16[8,1024]{1,0:T(8,128)(2,1)S(1)}, u32[]{:S(2)}, u32[]{:S(2)}) %collective-permute-start.6) | collective-permute-done | bytes 16416 | tf_op jit(solution)/shard_map/ppermute | solution.py:35
  47.7 2.2 convolution_bitcast_fusion
  49.9 3.4 %all-to-all-start = ((f32[8,8,512]{2,1,0:T(8,128)}), f32[8,8,512]{2,1,0:T(8,128)S(1)}, u32[]{:S(2)}, u32[]{:S(2)}) async-start(f32[8,8,512]{2,1,0:T(8,128)} %convolution_bitcast_fusion), calls=%async_computation | async-start | bytes 262144 | tf_op jit(solution)/shard_map/all_to_all | solution.py:42
  53.3 0.8 fusion.80
  54.1 5.9 %all-to-all-done = f32[8,8,512]{2,1,0:T(8,128)S(1)} async-done(((f32[8,8,512]{2,1,0:T(8,128)}), f32[8,8,512]{2,1,0:T(8,128)S(1)}, u32[]{:S(2)}, u32[]{:S(2)}) %all-to-all-start) | async-done | bytes 131104 | tf_op jit(solution)/shard_map/all_to_all | solution.py:42
  60.0 0.6 copy-done.4
  60.7 41.9 %all-reduce.3.cloned.1.call-done = f32[8,4096]{1,0:T(8,128)} async-done(((f32[8,4096]{1,0:T(8,128)}), f32[8,4096]{1,0:T(8,128)}) %all-reduce.3.cloned.1.call-update) | async-done | bytes 131088 | tf_op jit(solution)/shard_map/psum | solution.py:43
  102.5 1.1 multiply_reduce_fusion
  103.6 1.0 multiply_convert_fusion
  104.6 14.7 %all_gather.3 = bf16[64,4096]{1,0:T(8,128)(2,1)S(1)} all-gather(bf16[8,4096]{1,0:T(8,128)(2,1)S(1)} %multiply_convert_fusion), channel_id=1, replica_groups=mesh['expert'=4,'shard'=8] {'shard'}, dimensions={0}, use_global_device_ids=true | all-gather | bytes 589824 | tf_op jit(solution)/shard_map/all_gather | solution.py:47
  119.3 6.5 %fusion.5 = f32[64,1792]{1,0:T(8,128)S(1)} fusion(bf16[64,4096]{1,0:T(8,128)(2,1)S(1)} %all_gather.3, bf16[2,4096,1792]{2,1,0:T(8,128)(2,1)} %param.21), kind=kOutput, calls=%fused_computation.7 | convolution fusion | flops 939524096 | bytes 15663104 | tf_op jit(solution)/shard_map/dot_general | solution.py:64
  125.8 6.4 %fusion.11 = f32[64,1792]{1,0:T(8,128)S(1)} fusion(bf16[64,4096]{1,0:T(8,128)(2,1)S(1)} %all_gather.3, bf16[2,4096,1792]{2,1,0:T(8,128)(2,1)} %param.21), kind=kOutput, calls=%fused_computation.13 | convolution fusion | flops 939524096 | bytes 15663104 | tf_op jit(solution)/shard_map/dot_general | solution.py:64
  132.3 0.2 fusion.82
  132.5 0.7 gather_fusion
  133.3 0.7 gather_fusion.1
  134.1 13.1 %fusion.25 = f32[64,4096]{1,0:T(8,128)} fusion(bf16[2,1792,4096]{2,1,0:T(8,128)(2,1)} %param.23, bf16[64,4096]{1,0:T(8,128)(2,1)S(1)} %all_gather.3, bf16[2,4096,1792]{2,1,0:T(8,128)(2,1)} %param.22, f32[64]{0:T(128)S(1)} %fusion.74, f32[64,1792]{1,0:T(8,128)S(1)} %fusion.5), kind=kOutput, calls=%fused_computation.23 | convolution fusion | flops 1879998464 | bytes 31392000 | tf_op jit(solution)/shard_map/dot_general | solution.py:67
  147.2 13.6 %fusion.22 = f32[64,4096]{1,0:T(8,128)} fusion(f32[64,4096]{1,0:T(8,128)} %fusion.25, bf16[2,1792,4096]{2,1,0:T(8,128)(2,1)} %param.23, bf16[64,4096]{1,0:T(8,128)(2,1)S(1)} %all_gather.3, bf16[2,4096,1792]{2,1,0:T(8,128)(2,1)} %param.22, f32[64]{0:T(128)S(1)} %get-tuple-element.6, f32[64,1792]{1,0:T(8,128)S(1)} %fusion.11), kind=kOutput, calls=%fused_computation.22 | convolution fusion | flops 1880260608 | bytes 32440576 | tf_op jit(solution)/shard_map/dot_general | solution.py:67
  160.9 32.9 %reduce-scatter.2.cloned.1.call-done = f32[8,4096]{1,0:T(8,128)} async-done(((f32[64,4096]{1,0:T(8,128)}), f32[8,4096]{1,0:T(8,128)}) %reduce-scatter.2.cloned.1.call-update) | async-done | bytes 131088 | tf_op jit(solution)/shard_map/reduce_scatter | solution.py:69
  193.8 43.4 %all-reduce.5.cloned.1.call-done = f32[8,4096]{1,0:T(8,128)} async-done(((f32[8,4096]{1,0:T(8,128)}), f32[8,4096]{1,0:T(8,128)}) %all-reduce.5.cloned.1.call-update) | async-done | bytes 131088 | tf_op jit(solution)/shard_map/psum | solution.py:70
  237.1 1.6 add_convert_fusion
  (48 shorter events, 0.4 us)
Async XLA Ops:
  6.5 1.6 copy-start
  11.8 6.0 %collective-permute-start = (bf16[8,1024]{1,0:T(8,128)(2,1)S(1)}, bf16[8,1024]{1,0:T(8,128)(2,1)S(1)}, u32[]{:S(2)}, u32[]{:S(2)}) collective-permute-start(bf16[8,1024]{1,0:T(8,128)(2,1)S(1)} %reshape.37), channel_id=1, source_target_pairs={{0,1},{1,2},{2,3},{3,4},{4,5},{5,6},{6,7},{7,0},{8,9},{9,10},{10,1... | collective-permute-start | bytes 49160 | tf_op jit(solution)/shard_map/ppermute | solution.py:35
  17.8 5.0 %collective-permute-start.1 = (bf16[8,1024]{1,0:T(8,128)(2,1)S(1)}, bf16[8,1024]{1,0:T(8,128)(2,1)S(1)}, u32[]{:S(2)}, u32[]{:S(2)}) collective-permute-start(bf16[8,1024]{1,0:T(8,128)(2,1)S(1)} %collective-permute-done), channel_id=1, source_target_pairs={{0,1},{1,2},{2,3},{3,4},{4,5},{5,6},{6,7},{7,0},{8,9},{9,10},{10,1... | collective-permute-start | bytes 49160 | tf_op jit(solution)/shard_map/ppermute | solution.py:35
  22.7 5.0 %collective-permute-start.2 = (bf16[8,1024]{1,0:T(8,128)(2,1)S(1)}, bf16[8,1024]{1,0:T(8,128)(2,1)S(1)}, u32[]{:S(2)}, u32[]{:S(2)}) collective-permute-start(bf16[8,1024]{1,0:T(8,128)(2,1)S(1)} %collective-permute-done.1), channel_id=1, source_target_pairs={{0,1},{1,2},{2,3},{3,4},{4,5},{5,6},{6,7},{7,0},{8,9},{9,10},{10,1... | collective-permute-start | bytes 49160 | tf_op jit(solution)/shard_map/ppermute | solution.py:35
  27.7 5.0 %collective-permute-start.3 = (bf16[8,1024]{1,0:T(8,128)(2,1)S(1)}, bf16[8,1024]{1,0:T(8,128)(2,1)S(1)}, u32[]{:S(2)}, u32[]{:S(2)}) collective-permute-start(bf16[8,1024]{1,0:T(8,128)(2,1)S(1)} %collective-permute-done.2), channel_id=1, source_target_pairs={{0,1},{1,2},{2,3},{3,4},{4,5},{5,6},{6,7},{7,0},{8,9},{9,10},{10,1... | collective-permute-start | bytes 49160 | tf_op jit(solution)/shard_map/ppermute | solution.py:35
  32.7 5.0 %collective-permute-start.4 = (bf16[8,1024]{1,0:T(8,128)(2,1)S(1)}, bf16[8,1024]{1,0:T(8,128)(2,1)S(1)}, u32[]{:S(2)}, u32[]{:S(2)}) collective-permute-start(bf16[8,1024]{1,0:T(8,128)(2,1)S(1)} %collective-permute-done.3), channel_id=1, source_target_pairs={{0,1},{1,2},{2,3},{3,4},{4,5},{5,6},{6,7},{7,0},{8,9},{9,10},{10,1... | collective-permute-start | bytes 49160 | tf_op jit(solution)/shard_map/ppermute | solution.py:35
  37.6 5.0 %collective-permute-start.5 = (bf16[8,1024]{1,0:T(8,128)(2,1)S(1)}, bf16[8,1024]{1,0:T(8,128)(2,1)S(1)}, u32[]{:S(2)}, u32[]{:S(2)}) collective-permute-start(bf16[8,1024]{1,0:T(8,128)(2,1)S(1)} %collective-permute-done.4), channel_id=1, source_target_pairs={{0,1},{1,2},{2,3},{3,4},{4,5},{5,6},{6,7},{7,0},{8,9},{9,10},{10,1... | collective-permute-start | bytes 49160 | tf_op jit(solution)/shard_map/ppermute | solution.py:35
  42.6 5.0 %collective-permute-start.6 = (bf16[8,1024]{1,0:T(8,128)(2,1)S(1)}, bf16[8,1024]{1,0:T(8,128)(2,1)S(1)}, u32[]{:S(2)}, u32[]{:S(2)}) collective-permute-start(bf16[8,1024]{1,0:T(8,128)(2,1)S(1)} %collective-permute-done.5), channel_id=1, source_target_pairs={{0,1},{1,2},{2,3},{3,4},{4,5},{5,6},{6,7},{7,0},{8,9},{9,10},{10,1... | collective-permute-start | bytes 49160 | tf_op jit(solution)/shard_map/ppermute | solution.py:35
  49.9 10.1 %all-to-all-start = ((f32[8,8,512]{2,1,0:T(8,128)}), f32[8,8,512]{2,1,0:T(8,128)S(1)}, u32[]{:S(2)}, u32[]{:S(2)}) async-start(f32[8,8,512]{2,1,0:T(8,128)} %convolution_bitcast_fusion), calls=%async_computation | async-start | bytes 262144 | tf_op jit(solution)/shard_map/all_to_all | solution.py:42
  53.3 49.3 %all-reduce.3.cloned.1.call-start = ((), (), s32[]{:S(2)}) async-start(), calls=%async_computation.2 | async-start | bytes 262144 | tf_op jit(solution)/shard_map/psum | solution.py:43
  60.0 0.6 copy-start.4
  60.6 133.1 %reduce-scatter.2.cloned.1.call-start = ((), (), s32[]{:S(2)}) async-start(), calls=%async_computation.3 | async-start | bytes 1179648 | tf_op jit(solution)/shard_map/reduce_scatter | solution.py:69
  119.3 12.9 %copy-start.5 = (bf16[4096,8]{0,1:T(8,128)(2,1)S(1)}, bf16[4096,8]{0,1:T(8,128)(2,1)}, u32[]{:S(2)}) copy-start(bf16[4096,8]{0,1:T(8,128)(2,1)} %param.19) | copy-start | bytes 196612
  119.3 14.7 %copy-start.6 = (s32[64,2]{0,1:T(2,128)S(1)}, s32[64,2]{0,1:T(2,128)}, u32[]{:S(2)}) copy-start(s32[64,2]{0,1:T(2,128)} %param.20) | copy-start | bytes 1540
  147.2 91.5 %copy-start.1 = (bf16[8,512,2,128]{3,2,1,0:T(2,128)(2,1)S(1)}, bf16[8,512,2,128]{3,2,1,0:T(2,128)(2,1)}, u32[]{:S(2)}) copy-start(bf16[8,512,2,128]{3,2,1,0:T(2,128)(2,1)} %param.15) | copy-start | bytes 6291460
  147.2 89.9 %copy-start.2 = (f32[8,4096]{1,0:T(8,128)S(1)}, f32[8,4096]{1,0:T(8,128)}, u32[]{:S(2)}) copy-start(f32[8,4096]{1,0:T(8,128)} %all-reduce.3.cloned.1.call-done) | copy-start | bytes 393220
  147.2 89.9 %copy-start.3 = (bf16[8,4096]{1,0:T(8,128)(2,1)S(1)}, bf16[8,4096]{1,0:T(8,128)(2,1)}, u32[]{:S(2)}) copy-start(bf16[8,4096]{1,0:T(8,128)(2,1)} %param.13) | copy-start | bytes 196612
  160.8 76.3 %all-reduce.5.cloned.1.call-start = ((), (), s32[]{:S(2)}) async-start(), calls=%async_computation.4 | async-start | bytes 262144 | tf_op jit(solution)/shard_map/psum | solution.py:70
Sparse Core Ops, SparseCore 0:
  60.7 41.7 all-reduce.2
  160.9 32.7 reduce-scatter.1
  196.6 40.4 all-reduce.4
